TPU v7x, 32 devices: a whole 2x2x4 slice. The times are simulated.
32 devices in a mesh: row: 8 (over y, x, core), col: 4 (over z).
Axes of the slice: x: 2, y: 2, z: 4, core: 2. Of those that a mesh axis runs over, the one named last changes fastest.
Arguments:
- a_blocks: bfloat16 [1024, 16, 128, 128], P(('row', 'col')), may hold values from -0.0625 to 0.0625
- omega: bfloat16 [16384, 256], P('col'), may hold values from -6 to 6
- route_dest: int32 [1024, 1], P(('row', 'col')), may hold values from 0 to 7; in each aligned block of 32 rows (0 to 31, 32 to 63, ...) at most 4 rows name the same one
- row_target: int32 [1024], P(('row', 'col')), may hold values from 0 to 31
- col_target: int32 [1024, 16], P(('row', 'col')), may hold values from 0 to 31
Outputs:
- basis: float32 [32768, 256], P(('row', 'col'))
- factor: float32 [256, 256], replicated
Inputs may be any that keep to these rules, and one draw needn't show every extreme that they name: `route_dest`: among the 32 rows of one device no value appears more than 4 times, and in some device's rows one value appears exactly 4 times.
All inputs are finite; a program needn't handle non-finite values.
Results may differ from a plain program's by a relative error of at most 0.003.
Values may be sent and summed in bfloat16 or wider, within the bound.
A program may use at most 192 MiB of HBM per device.

v0:
```python
import jax
import jax.numpy as jnp
from jax import lax
from jax.sharding import PartitionSpec as P

RB_DEV = 8
CAP = 4


def product(left, right):
    return jnp.dot(left, right, precision=lax.Precision.HIGHEST, preferred_element_type=jnp.float32)


def upper_factor(gram):
    order = gram.shape[0]
    lower = jnp.linalg.cholesky(gram)
    identity = jnp.eye(order, dtype=jnp.float32)
    inverse = jax.scipy.linalg.solve_triangular(lower, identity, lower=True)
    return (lower.T, inverse.T)


def body(a_blocks, omega, route_dest, row_target, col_target):
    targets_here, group_size, block_order, _ = a_blocks.shape
    sketch_width = omega.shape[1]
    row_count = lax.axis_size("row")
    slab = omega.reshape(omega.shape[0] // block_order, block_order, sketch_width)
    picked = slab[col_target]
    partial_value = jnp.einsum(
        "tgij,tgjk->tik", a_blocks, picked, preferred_element_type=jnp.float32
    ).astype(jnp.bfloat16)
    destination = route_dest[:, 0]
    positions = jnp.arange(targets_here, dtype=jnp.int32)
    same_owner = destination[:, None] == destination[None, :]
    earlier = positions[None, :] < positions[:, None]
    rank = jnp.sum(jnp.logical_and(same_owner, earlier), axis=1)
    slot_of = destination * CAP + rank
    slot_ids = jnp.arange(row_count * CAP, dtype=jnp.int32)
    matches = slot_of[None, :] == slot_ids[:, None]
    filled = jnp.any(matches, axis=1)
    source = jnp.sum(jnp.where(matches, positions[None, :], 0), axis=1)
    send_values = jnp.where(
        filled[:, None, None], partial_value[source], jnp.zeros((), jnp.bfloat16)
    )
    send_values = send_values.reshape(row_count, CAP, block_order, sketch_width)
    send_rows = jnp.where(filled, row_target[source], -1).reshape(row_count, CAP)
    got_values, got_rows = (
        lax.all_to_all(send_values, "row", split_axis=0, concat_axis=0, tiled=True),
        lax.all_to_all(send_rows, "row", split_axis=0, concat_axis=0, tiled=True),
    )
    flat_values = got_values.reshape(row_count * CAP, block_order, sketch_width)
    flat_rows = got_rows.reshape(row_count * CAP)
    count = lax.axis_size("col") * (RB_DEV * block_order)
    block_total = count // block_order
    wanted = jnp.arange(block_total, dtype=jnp.int32)
    selector = (flat_rows[None, :] == wanted[:, None]).astype(jnp.bfloat16)
    term = jnp.einsum("bs,sik->bik", selector, flat_values, preferred_element_type=jnp.float32)
    sketch = lax.psum_scatter(
        term.reshape(count, sketch_width), "col", scatter_dimension=0, tiled=True
    )
    gram_one = lax.psum(product(sketch.T, sketch), ("row", "col"))
    first, first_inv = upper_factor(gram_one)
    once = product(sketch, first_inv)
    gram_two = lax.psum(product(once.T, once), ("row", "col"))
    second, second_inv = upper_factor(gram_two)
    basis = product(once, second_inv)
    factor = product(second, first)
    total_rows = float(sketch.shape[0] * lax.axis_size(("row", "col")))
    scale_root = jnp.sqrt(jnp.float32(total_rows))
    return (basis * scale_root, factor / scale_root)


def solution(mesh):
    return jax.shard_map(
        body,
        mesh=mesh,
        in_specs=(
            P(("row", "col"), None, None, None),
            P("col", None),
            P(("row", "col"), None),
            P(("row", "col")),
            P(("row", "col"), None),
        ),
        out_specs=(P(("row", "col"), None), P()),
        check_vma=False,
    )
```

profile of v0, /device:TPU:0, one launch (start us, length us, event | category | flops | bytes accessed | tf_op | source)
XLA Modules:
  0.0 578.0 jit_solution(14751288368338231780)
XLA Ops:
  7.2 1.0 convert_reduce_fusion
  8.2 0.7 multiply_add_fusion
  9.1 1.4 gather_fusion
  10.5 0.7 select_n.44
  11.1 5.2 all-to-all-start
  16.4 0.7 compare_select_fusion
  17.3 16.1 %gather_fusion.1 = bf16[512,128,256]{2,1,0:T(8,128)(2,1)} fusion(bf16[32,128,256]{2,1,0:T(8,128)(2,1)S(1)} %bitcast.94, s32[1024]{0:T(1024)S(1)} %pad_clamp_fusion), kind=kCustom, calls=%fused_computation.1 | custom fusion | bytes 67110912 | tf_op jit(solution)/shard_map/gather | solution.py:27
  33.4 19.5 %fusion = bf16[32,128,256]{1,2,0:T(8,128)(2,1)} fusion(bf16[32,16,128,256]{3,2,1,0:T(8,128)(2,1)} %bitcast.95, bf16[32,16,128,128]{3,2,1,0:T(8,128)(2,1)} %param.8), kind=kOutput, calls=%fused_computation.9 | convolution fusion | flops 4296015872 | bytes 52428800 | tf_op jit(solution)/shard_map/tgij,tgjk->tik/dot_general | solution.py:28
  52.9 2.5 gather_fusion.2
  55.5 1.6 broadcast_select_fusion
  57.0 4.1 all-to-all-start.1
  61.2 0.5 broadcast.141
  61.7 0.7 reduce.11
  62.5 25.3 %all-to-all-done.1 = bf16[8,4,128,256]{2,3,1,0:T(8,128)(2,1)S(1)} async-done(((bf16[8,4,128,256]{2,3,1,0:T(8,128)(2,1)}), bf16[8,4,128,256]{2,3,1,0:T(8,128)(2,1)S(1)}, u32[]{:S(2)}, u32[]{:S(2)}) %all-to-all-start.1) | async-done | bytes 2097184 | tf_op jit(solution)/shard_map/all_to_all | solution.py:47
  87.8 1.3 copy-done.3
  89.1 3.4 copy.42
  92.5 0.7 fusion.36
  93.2 4.4 copy.34
  97.6 76.3 %reduce-scatter.2.cloned.1.call-done = f32[1024,256]{1,0:T(8,128)} async-done(((f32[4096,256]{1,0:T(8,128)}), f32[1024,256]{1,0:T(8,128)}) %reduce-scatter.2.cloned.1.call-update) | async-done | bytes 1048592 | tf_op jit(solution)/shard_map/reduce_scatter | solution.py:57
  173.9 4.1 fusion.46
  178.0 0.2 all-reduce.6.cloned.1.call-start
  178.3 128.9 %all-reduce.4.cloned.1.call-done = f32[256,256]{0,1:T(8,128)} async-done(((f32[256,256]{0,1:T(8,128)}), f32[256,256]{0,1:T(8,128)}) %all-reduce.4.cloned.1.call-update) | async-done | bytes 262160 | tf_op jit(solution)/shard_map/psum | solution.py:60
  307.2 1.1 copy.36
  308.3 1.0 fusion.9
  309.3 11.7 %cholesky.130 = f32[128,128]{1,0:T(8,128)S(1)} custom-call(f32[128,128]{1,0:T(8,128)S(1)} %cholesky.194), custom_call_target="Cholesky" | custom-call | tf_op jit(solution)/shard_map/jit(cholesky)/cholesky | solution.py:16
  321.1 9.8 %custom-call.13 = f32[1,128,128]{1,2,0:T(8,128)S(1)} custom-call(f32[1,128,128]{2,1,0:T(8,128)S(1)} %get-tuple-element.47), custom_call_target="InvertDiagBlocksLowerTriangular" | custom-call | tf_op jit(solution)/shard_map/jit(cholesky)/cholesky | solution.py:16
  330.9 0.2 constant_dynamic-update-slice_fusion.3
  331.1 0.3 convolution_subtract_fusion.3
  331.4 11.7 %cholesky.147 = f32[128,128]{1,0:T(8,128)S(1)} custom-call(f32[128,128]{1,0:T(8,128)S(1)} %convolution_subtract_fusion.3), custom_call_target="Cholesky" | custom-call | tf_op jit(solution)/shard_map/jit(cholesky)/cholesky | solution.py:16
  343.1 0.7 compare_reduce_fusion.2
  345.3 4.1 while.4
  345.3 0.6 fusion.67
  345.9 1.4 bitcast_dynamic-update-slice_fusion.4
  347.4 0.6 fusion.67
  348.0 1.4 bitcast_dynamic-update-slice_fusion.4
  349.4 19.9 %custom-call.14 = f32[2,128,128]{1,2,0:T(8,128)S(1)} custom-call(f32[2,128,128]{2,1,0:T(8,128)S(1)} %get-tuple-element.18), custom_call_target="InvertDiagBlocksLowerTriangular" | custom-call | tf_op jit(solution)/shard_map/jit(_solve_triangular)/triangular_solve | solution.py:18
  369.3 0.3 fusion.21
  369.6 0.3 convolution_subtract_fusion.1
  369.9 0.3 fusion.28
  370.2 1.0 fusion.1
  371.3 2.5 fusion.47
  373.8 125.8 %all-reduce.6.cloned.1.call-done = f32[256,256]{0,1:T(8,128)} async-done(((f32[256,256]{0,1:T(8,128)}), f32[256,256]{0,1:T(8,128)}) %all-reduce.6.cloned.1.call-update) | async-done | bytes 262160 | tf_op jit(solution)/shard_map/psum | solution.py:63
  499.6 1.1 copy.38
  500.7 1.0 fusion.8
  501.7 11.7 %cholesky.164 = f32[128,128]{1,0:T(8,128)S(1)} custom-call(f32[128,128]{1,0:T(8,128)S(1)} %cholesky.197), custom_call_target="Cholesky" | custom-call | tf_op jit(solution)/shard_map/jit(cholesky)/cholesky | solution.py:16
  513.5 9.8 %custom-call.15 = f32[1,128,128]{1,2,0:T(8,128)S(1)} custom-call(f32[1,128,128]{2,1,0:T(8,128)S(1)} %get-tuple-element.43), custom_call_target="InvertDiagBlocksLowerTriangular" | custom-call | tf_op jit(solution)/shard_map/jit(cholesky)/cholesky | solution.py:16
  523.3 0.2 constant_dynamic-update-slice_fusion.1
  523.5 0.3 convolution_subtract_fusion.2
  523.8 11.9 %cholesky.181 = f32[128,128]{1,0:T(8,128)S(1)} custom-call(f32[128,128]{1,0:T(8,128)S(1)} %convolution_subtract_fusion.2), custom_call_target="Cholesky" | custom-call | tf_op jit(solution)/shard_map/jit(cholesky)/cholesky | solution.py:16
  535.7 0.6 compare_reduce_fusion.1
  536.4 0.6 compare_reduce_fusion
  538.3 0.7 fusion.10
  539.1 1.2 convolution_multiply_fusion.1
  540.3 5.8 %while.5 = (s32[]{:T(128)}, f32[256,256]{1,0:T(8,128)}, s32[2,2]{1,0:T(2,128)S(1)}, f32[2,128,128]{2,1,0:T(8,128)S(1)}, s32[]{:T(128)}) while((s32[]{:T(128)}, f32[256,256]{1,0:T(8,128)}, s32[2,2]{1,0:T(2,128)S(1)}, f32[2,128,128]{2,1,0:T(8,128)S(1)}, s32[]{:T(128)}) %tuple.59), condition=%wide.while_cond.clone, body=%wide.while_body.clone.sunk | while | flops 2 | bytes 131189 | solution.py:18
  540.3 0.7 fusion.68
  541.0 2.2 bitcast_dynamic-update-slice_fusion.5
  543.3 0.7 fusion.68
  543.9 2.2 bitcast_dynamic-update-slice_fusion.5
  546.1 0.6 copy-done.4
  546.8 20.5 %custom-call.16 = f32[2,128,128]{1,2,0:T(8,128)S(1)} custom-call(f32[2,128,128]{2,1,0:T(8,128)} %copy-done.4), custom_call_target="InvertDiagBlocksLowerTriangular" | custom-call | tf_op jit(solution)/shard_map/jit(_solve_triangular)/triangular_solve | solution.py:18
  567.3 0.3 fusion.19
  567.6 1.1 convolution_subtract_fusion
  568.7 0.3 fusion.24
  569.0 2.0 convolution_multiply_fusion
  (42 shorter events, 1.1 us)
Async XLA Ops:
  7.2 10.1 %copy-start = (bf16[4096,256]{1,0:T(8,128)(2,1)S(1)}, bf16[4096,256]{1,0:T(8,128)(2,1)}, u32[]{:S(2)}) copy-start(bf16[4096,256]{1,0:T(8,128)(2,1)} %param.9) | copy-start | bytes 6291460
  11.1 45.9 %all-to-all-start = ((s32[8,1,4]{2,1,0:T(1,128)}), s32[8,1,4]{2,1,0:T(1,128)S(1)}, u32[]{:S(2)}, u32[]{:S(2)}) async-start(s32[8,1,4]{2,1,0:T(1,128)} %bitcast.3), calls=%async_computation | async-start | bytes 8192 | tf_op jit(solution)/shard_map/all_to_all | solution.py:48
  57.0 30.7 %all-to-all-start.1 = ((bf16[8,4,128,256]{2,3,1,0:T(8,128)(2,1)}), bf16[8,4,128,256]{2,3,1,0:T(8,128)(2,1)S(1)}, u32[]{:S(2)}, u32[]{:S(2)}) async-start(bf16[8,4,128,256]{2,3,1,0:T(8,128)(2,1)} %broadcast_select_fusion), calls=%async_computation.1 | async-start | bytes 4194304 | tf_op jit(solution)/shard_map/all_to_all | solution.py:47
  61.1 112.8 %reduce-scatter.2.cloned.1.call-start = ((), (), s32[]{:S(2)}) async-start(), calls=%async_computation.3 | async-start | bytes 5242880 | tf_op jit(solution)/shard_map/reduce_scatter | solution.py:57
  87.8 1.4 copy-start.3
  97.6 209.6 %all-reduce.4.cloned.1.call-start = ((), (), s32[]{:S(2)}) async-start(), calls=%async_computation.4 | async-start | bytes 524288 | tf_op jit(solution)/shard_map/psum | solution.py:60
  178.0 321.6 %all-reduce.6.cloned.1.call-start = ((), (), s32[]{:S(2)}) async-start(), calls=%async_computation.5 | async-start | bytes 524288 | tf_op jit(solution)/shard_map/psum | solution.py:63
  309.3 61.0 %copy-start.2 = (f32[1024,256]{1,0:T(8,128)S(1)}, f32[1024,256]{1,0:T(8,128)}, u32[]{:S(2)}) copy-start(f32[1024,256]{1,0:T(8,128)} %reduce-scatter.2.cloned.1.call-done) | copy-start | bytes 3145732
  540.3 30.7 %copy-start.1 = (bf16[4096,256]{1,0:T(8,128)(2,1)S(1)}, bf16[4096,256]{1,0:T(8,128)(2,1)}, u32[]{:S(2)}) copy-start(bf16[4096,256]{1,0:T(8,128)(2,1)} %param.9) | copy-start | bytes 6291460
  546.1 0.6 copy-start.4
Sparse Core Ops, SparseCore 0:
  97.7 76.1 reduce-scatter.1
  180.0 127.1 all-reduce.3
  373.9 125.6 all-reduce.5
where the time goes:
time: 587 us; the launch traced here: 578 us
  waiting for transfers between devices  356 us (61%)
  other arithmetic  117 us (20%)
  local copies, waits for them, and re-layouts  43.4 us (7%)
  matrix products  34.5 us (6%)
  between operations  17.1 us (3%)
  starting transfers between devices  9.61 us (2%)
    psum x1, waiting for transfers between devices, body(): gram_one = lax.psum(product(sketch.T, sketch), ('row', 'col'))  129 us
    psum x1, waiting for transfers between devices, body(): gram_two = lax.psum(product(once.T, once), ('row', 'col'))  126 us
    reduce_scatter x1, waiting for transfers between devices, body(): lax.psum_scatter(term.reshape(count, sketch_width), 'col', scatter_dimens...  76.3 us
    another operation x13, other arithmetic, upper_factor(): lower = jnp.linalg.cholesky(gram)  68.8 us
    another operation x5, other arithmetic, upper_factor(): inverse = jax.scipy.linalg.solve_triangular(lower, identity, lower=True)  41.1 us
    all_to_all x1, waiting for transfers between devices, body(): lax.all_to_all(send_values, 'row', split_axis=0, concat_axis=0, tiled=True)  25.3 us
    dot_general x1, matrix products, body(): jnp.einsum('tgij,tgjk->tik', a_blocks, picked, preferred_element_type=jnp...  19.5 us
    gather x1, local copies, waits for them, and re-layouts, body(): picked = slab[col_target]  16.1 us
  transfers between devices with their start and end apart: 5, of which 4 were waited for; matrix products, arithmetic and copies ran while one was open for 7% of the time, Pallas kernels for 0%

commit v1 on v0

v1 whole, which is shorter than its diff:
```python
import functools

import jax
import jax.numpy as jnp
from jax import lax
from jax.experimental import pallas as pl
from jax.experimental.pallas import tpu as pltpu
from jax.sharding import PartitionSpec as P

RB_DEV = 8
CAP = 4
PANEL = 64
MESH = pl.DeviceIdType.MESH
ANY = pl.BlockSpec(memory_space=pl.ANY)
VMEM = pl.BlockSpec(memory_space=pltpu.VMEM)
SMEM = pl.BlockSpec(memory_space=pltpu.SMEM)
HIGH = lax.Precision.HIGHEST


def dot_nn(a, b):
    return lax.dot_general(a, b, (((1,), (0,)), ((), ())), precision=HIGH, preferred_element_type=jnp.float32)


def dot_nt(a, b):
    return lax.dot_general(a, b, (((1,), (1,)), ((), ())), precision=HIGH, preferred_element_type=jnp.float32)


def dot_tn(a, b):
    return lax.dot_general(a, b, (((0,), (0,)), ((), ())), precision=HIGH, preferred_element_type=jnp.float32)


def partial_kernel(slot_ref, col_ref, a_ref, omega_ref, out_ref):
    step = pl.program_id(0)
    per_step, groups, order, _ = a_ref.shape
    for local in range(per_step):
        t = step * per_step + local
        total = None
        for g in range(0, groups, 2):
            left = jnp.concatenate([a_ref[local, g], a_ref[local, g + 1]], axis=1)
            c0 = pl.multiple_of(col_ref[t * groups + g] * order, order)
            c1 = pl.multiple_of(col_ref[t * groups + g + 1] * order, order)
            right = jnp.concatenate([omega_ref[pl.ds(c0, order), :], omega_ref[pl.ds(c1, order), :]], axis=0)
            term = jnp.dot(left, right, preferred_element_type=jnp.float32)
            total = term if total is None else total + term
        out_ref[slot_ref[t]] = total.astype(jnp.bfloat16)


def partials(slot_of, col_flat, a_blocks, omega, slots):
    targets, groups, order, _ = a_blocks.shape
    width = omega.shape[1]
    per_step = 4
    return pl.pallas_call(
        partial_kernel,
        out_shape=jax.ShapeDtypeStruct((slots, order, width), jnp.bfloat16),
        grid_spec=pltpu.PrefetchScalarGridSpec(
            num_scalar_prefetch=2,
            grid=(targets // per_step,),
            in_specs=[
                pl.BlockSpec((per_step, groups, order, order), lambda i, *_: (i, 0, 0, 0)),
                pl.BlockSpec(omega.shape, lambda i, *_: (0, 0)),
            ],
            out_specs=pl.BlockSpec((slots, order, width), lambda i, *_: (0, 0, 0)),
        ),
        compiler_params=pltpu.CompilerParams(vmem_limit_bytes=40 << 20),
    )(slot_of, col_flat, a_blocks, omega)


def row_exchange_kernel(nr, send_ref, srow_ref, got_ref, grow_ref, s_sem, r_sem, s2_sem, r2_sem, own_sem):
    r = lax.axis_index("row")
    c = lax.axis_index("col")
    barrier = pltpu.get_barrier_semaphore()
    for k in range(1, nr):
        pl.semaphore_signal(barrier, inc=1, device_id=(lax.rem(r + k, nr), c), device_id_type=MESH)
    own = pltpu.make_async_copy(send_ref.at[r], got_ref.at[r], own_sem.at[0])
    own_rows = pltpu.make_async_copy(srow_ref.at[r], grow_ref.at[r], own_sem.at[1])
    own.start()
    own_rows.start()
    pl.semaphore_wait(barrier, nr - 1)
    copies = []
    for k in range(1, nr):
        d = lax.rem(r + k, nr)
        for src, dst, ss, rs in ((srow_ref, grow_ref, s2_sem, r2_sem), (send_ref, got_ref, s_sem, r_sem)):
            cp = pltpu.make_async_remote_copy(src.at[d], dst.at[r], ss.at[k], rs.at[k], device_id=(d, c), device_id_type=MESH)
            cp.start()
            copies.append(cp)
    own.wait()
    own_rows.wait()
    for cp in copies:
        cp.wait()


def row_exchange(send, rows, nr):
    dma = pltpu.SemaphoreType.DMA
    return pl.pallas_call(
        functools.partial(row_exchange_kernel, nr),
        out_shape=(jax.ShapeDtypeStruct(send.shape, send.dtype), jax.ShapeDtypeStruct(rows.shape, rows.dtype)),
        in_specs=[ANY, ANY],
        out_specs=(ANY, ANY),
        scratch_shapes=[dma((nr,)), dma((nr,)), dma((nr,)), dma((nr,)), dma((2,))],
        compiler_params=pltpu.CompilerParams(collective_id=1, has_side_effects=True),
    )(send, rows)


def gather_sum_kernel(rows_ref, me_ref, got_ref, term_ref, own_ref, acc):
    acc[...] = jnp.zeros_like(acc)

    @pl.loop(0, got_ref.shape[0])
    def _(s):
        row = rows_ref[s]

        @pl.when(row >= 0)
        def _():
            acc[row] = acc[row] + got_ref[s].astype(jnp.float32)

    @pl.loop(0, acc.shape[0])
    def _(b):
        term_ref[b] = acc[b].astype(jnp.bfloat16)

    @pl.loop(0, own_ref.shape[0])
    def _(b):
        own_ref[b] = acc[me_ref[0] * own_ref.shape[0] + b]


def gather_sum(rows, me, got, blocks):
    _, order, width = got.shape
    return pl.pallas_call(
        gather_sum_kernel,
        out_shape=(
            jax.ShapeDtypeStruct((blocks, order, width), jnp.bfloat16),
            jax.ShapeDtypeStruct((RB_DEV, order, width), jnp.float32),
        ),
        in_specs=[SMEM, SMEM, VMEM],
        out_specs=(VMEM, VMEM),
        scratch_shapes=[pltpu.VMEM((blocks, order, width), jnp.float32)],
        compiler_params=pltpu.CompilerParams(vmem_limit_bytes=48 << 20),
    )(rows, me, got)


def greet(nr, nc, r, c):
    barrier = pltpu.get_barrier_semaphore()
    for k in range(1, nr):
        pl.semaphore_signal(barrier, inc=1, device_id=(lax.rem(r + k, nr), c), device_id_type=MESH)
    for k in range(1, nc):
        pl.semaphore_signal(barrier, inc=1, device_id=(r, lax.rem(c + k, nc)), device_id_type=MESH)
    pl.semaphore_wait(barrier, nr - 1 + nc - 1)


def reduce_gram(nr, nc, r, c, gram, landed, cols, full, sems):
    a_s, a_r, b_s, b_r, c_s, c_r = sems
    chunk = gram.shape[0] // nr
    mine = pl.ds(pl.multiple_of(r * chunk, chunk), chunk)
    copies = []
    for k in range(1, nr):
        d = lax.rem(r + k, nr)
        cp = pltpu.make_async_remote_copy(
            gram.at[pl.ds(pl.multiple_of(d * chunk, chunk), chunk), :], landed.at[k], a_s.at[k], a_r.at[k],
            device_id=(d, c), device_id_type=MESH)
        cp.start()
        copies.append(cp)
    total = gram[mine, :]
    for k in range(1, nr):
        copies[k - 1].wait_recv()
        total = total + landed[k]
    cols[c] = total
    across = []
    for k in range(1, nc):
        cp = pltpu.make_async_remote_copy(
            cols.at[c], cols.at[c], b_s.at[k], b_r.at[k], device_id=(r, lax.rem(c + k, nc)), device_id_type=MESH)
        cp.start()
        across.append(cp)
    for cp in across:
        cp.wait_recv()
    total = cols[0]
    for k in range(1, nc):
        total = total + cols[k]
    full[mine, :] = total
    back = []
    for k in range(1, nr):
        cp = pltpu.make_async_remote_copy(
            full.at[mine, :], full.at[mine, :], c_s.at[k], c_r.at[k], device_id=(lax.rem(r + k, nr), c), device_id_type=MESH)
        cp.start()
        back.append(cp)
    for cp in back:
        cp.wait_recv()
    for cp in copies + across + back:
        cp.wait_send()


def gram_scratch(nr, nc, order):
    dma = pltpu.SemaphoreType.DMA
    chunk = order // nr
    return [
        pltpu.VMEM((nr, chunk, order), jnp.float32),
        pltpu.VMEM((nc, chunk, order), jnp.float32),
        pltpu.VMEM((order, order), jnp.float32),
        dma((nr,)), dma((nr,)), dma((nc,)), dma((nc,)), dma((nr,)), dma((nr,)),
    ]


def col_sum_kernel(nr, nc, term_ref, own_ref, sketch_ref, out_ref, got, gram, landed, cols, full, *sems):
    r = lax.axis_index("row")
    c = lax.axis_index("col")
    s_sem, r_sem = sems[6], sems[7]
    greet(nr, nc, r, c)
    copies = []
    for k in range(1, nc):
        d = lax.rem(c + k, nc)
        cp = pltpu.make_async_remote_copy(
            term_ref.at[pl.ds(d * RB_DEV, RB_DEV)], got.at[k], s_sem.at[k], r_sem.at[k],
            device_id=(r, d), device_id_type=MESH)
        cp.start()
        copies.append(cp)
    for cp in copies:
        cp.wait()
    order = own_ref.shape[1]
    gram[...] = jnp.zeros_like(gram)

    @pl.loop(0, RB_DEV // 2)
    def _(i):
        pieces = []
        for half in range(2):
            b = i * 2 + half
            total = own_ref[b]
            for k in range(1, nc):
                total = total + got[k, b].astype(jnp.float32)
            pieces.append(total)
        rows = jnp.concatenate(pieces, axis=0)
        sketch_ref[pl.ds(pl.multiple_of(i * 2 * order, 2 * order), 2 * order), :] = rows
        gram[...] += dot_tn(rows, rows)

    reduce_gram(nr, nc, r, c, gram, landed, cols, full, sems[:6])
    out_ref[...] = full[...]


def col_sum(term, own, nr, nc):
    _, order, width = own.shape
    dma = pltpu.SemaphoreType.DMA
    return pl.pallas_call(
        functools.partial(col_sum_kernel, nr, nc),
        out_shape=(
            jax.ShapeDtypeStruct((RB_DEV * order, width), jnp.float32),
            jax.ShapeDtypeStruct((width, width), jnp.float32),
        ),
        in_specs=[VMEM, VMEM],
        out_specs=(VMEM, VMEM),
        scratch_shapes=[
            pltpu.VMEM((nc, RB_DEV, order, width), jnp.bfloat16),
            pltpu.VMEM((width, width), jnp.float32),
        ] + gram_scratch(nr, nc, width) + [dma((nc,)), dma((nc,))],
        compiler_params=pltpu.CompilerParams(collective_id=2, has_side_effects=True, vmem_limit_bytes=48 << 20),
    )(term, own)


def gram_sum_kernel(nr, nc, gram, out_ref, landed, cols, full, *sems):
    r = lax.axis_index("row")
    c = lax.axis_index("col")
    greet(nr, nc, r, c)
    reduce_gram(nr, nc, r, c, gram, landed, cols, full, sems)
    out_ref[...] = full[...]


def gram_sum(gram, nr, nc):
    return pl.pallas_call(
        functools.partial(gram_sum_kernel, nr, nc),
        out_shape=jax.ShapeDtypeStruct(gram.shape, jnp.float32),
        in_specs=[VMEM],
        out_specs=VMEM,
        scratch_shapes=gram_scratch(nr, nc, gram.shape[0]),
        compiler_params=pltpu.CompilerParams(collective_id=3, has_side_effects=True),
    )(gram)


def eliminate(x):
    rows = x.shape[0]
    groups = [x[i:i + 8, :] for i in range(0, rows, 8)]
    sub = lax.broadcasted_iota(jnp.int32, (8, 1), 0)
    for j in range(rows - 1):
        g, o = divmod(j, 8)
        pivot_row = groups[g][o:o + 1, :]
        scaled = pivot_row * (1.0 / pivot_row[:, j:j + 1])
        for i in range(g, rows // 8):
            f = groups[i][:, j:j + 1]
            if i == g:
                if o == 7:
                    continue
                f = jnp.where(sub > o, f, 0.0)
            groups[i] = groups[i] - f * scaled
    return jnp.concatenate(groups, axis=0)


def factor_gram(gram, work, upper, inverse):
    order = gram.shape[0]
    row = lax.broadcasted_iota(jnp.int32, (order, order), 0)
    col = lax.broadcasted_iota(jnp.int32, (order, order), 1)
    work[:, :order] = gram[...]
    work[:, order:] = (row == col).astype(jnp.float32)
    lane = lax.broadcasted_iota(jnp.int32, (PANEL, 2 * PANEL), 1)
    prow = lax.broadcasted_iota(jnp.int32, (PANEL, 2 * PANEL), 0)

    @pl.loop(0, order // PANEL)
    def _(p):
        base = pl.multiple_of(p * PANEL, PANEL)
        tile = work[pl.ds(base, PANEL), pl.ds(pl.multiple_of((p // 2) * 2 * PANEL, 2 * PANEL), 2 * PANEL)]
        tile = jnp.where(p % 2 == 1, pltpu.roll(tile, PANEL, 1), tile)
        x = jnp.where(lane < PANEL, tile, (lane - PANEL == prow).astype(jnp.float32))
        x = eliminate(x)
        diag = jnp.sum(jnp.where(lane == prow, x, 0.0), axis=1, keepdims=True)
        left = pltpu.roll(x, PANEL, 1)[:, :PANEL]
        panel = dot_nn(left, work[pl.ds(base, PANEL), :])
        root = 1.0 / jnp.sqrt(diag)
        pcol = lax.broadcasted_iota(jnp.int32, (PANEL, order), 1)
        pr = lax.broadcasted_iota(jnp.int32, (PANEL, order), 0) + base
        upper[pl.ds(base, PANEL), :] = jnp.where(pcol >= pr, panel[:, :order] * root, 0.0)
        inverse[pl.ds(base, PANEL), :] = jnp.where(pcol <= pr, panel[:, order:] * root, 0.0)

        @pl.when(p < order // PANEL - 1)
        def _():
            half = panel * root
            update = dot_tn(half[:, :order], half)
            below = lax.broadcasted_iota(jnp.int32, (order, 1), 0) >= base + PANEL
            work[...] = jnp.where(below, work[...] - update, work[...])


def first_kernel(gram, sketch, upper, once, second, work, inverse):
    factor_gram(gram, work, upper, inverse)
    second[...] = jnp.zeros_like(second)
    step = 256

    @pl.loop(0, sketch.shape[0] // step)
    def _(i):
        part = pl.ds(pl.multiple_of(i * step, step), step)
        rows = dot_nt(sketch[part, :], inverse[...])
        once[part, :] = rows
        second[...] += dot_tn(rows, rows)


def first_pass(gram, sketch):
    order = gram.shape[0]
    square = jax.ShapeDtypeStruct((order, order), jnp.float32)
    return pl.pallas_call(
        first_kernel,
        out_shape=(square, jax.ShapeDtypeStruct(sketch.shape, jnp.float32), square),
        in_specs=[VMEM, VMEM],
        out_specs=(VMEM, VMEM, VMEM),
        scratch_shapes=[pltpu.VMEM((order, 2 * order), jnp.float32), pltpu.VMEM((order, order), jnp.float32)],
        compiler_params=pltpu.CompilerParams(vmem_limit_bytes=40 << 20),
    )(gram, sketch)


def last_kernel(scale, gram, once, upper_one, basis, factor, work, upper, inverse):
    factor_gram(gram, work, upper, inverse)
    factor[...] = dot_nn(upper[...], upper_one[...]) * (1.0 / scale)
    step = 256

    @pl.loop(0, once.shape[0] // step)
    def _(i):
        part = pl.ds(pl.multiple_of(i * step, step), step)
        basis[part, :] = dot_nt(once[part, :], inverse[...]) * scale


def last_pass(gram, once, upper_one, scale):
    order = gram.shape[0]
    square = pltpu.VMEM((order, order), jnp.float32)
    return pl.pallas_call(
        functools.partial(last_kernel, scale),
        out_shape=(
            jax.ShapeDtypeStruct(once.shape, jnp.float32),
            jax.ShapeDtypeStruct((order, order), jnp.float32),
        ),
        in_specs=[VMEM, VMEM, VMEM],
        out_specs=(VMEM, VMEM),
        scratch_shapes=[pltpu.VMEM((order, 2 * order), jnp.float32), square, square],
        compiler_params=pltpu.CompilerParams(vmem_limit_bytes=40 << 20),
    )(gram, once, upper_one)


def body(nr, nc, a_blocks, omega, route_dest, row_target, col_target):
    targets_here, _, order, _ = a_blocks.shape
    width = omega.shape[1]
    slots = nr * CAP
    destination = route_dest[:, 0]
    positions = jnp.arange(targets_here, dtype=jnp.int32)
    same_owner = destination[:, None] == destination[None, :]
    earlier = positions[None, :] < positions[:, None]
    rank = jnp.sum(jnp.logical_and(same_owner, earlier).astype(jnp.int32), axis=1)
    slot_of = destination * CAP + rank
    slot_ids = jnp.arange(slots, dtype=jnp.int32)
    matches = slot_of[None, :] == slot_ids[:, None]
    send_rows = jnp.sum(jnp.where(matches, row_target[None, :] + 1, 0), axis=1) - 1
    send_rows = jnp.pad(send_rows.reshape(nr, 1, CAP), ((0, 0), (0, 0), (0, 128 - CAP)))
    send_rows = jnp.broadcast_to(send_rows, (nr, 8, 128))
    send = partials(slot_of, col_target.reshape(-1), a_blocks, omega, slots)
    got, got_rows = row_exchange(send.reshape(nr, CAP, order, width), send_rows, nr)
    me = lax.axis_index("col").astype(jnp.int32).reshape(1)
    term, own = gather_sum(got_rows[:, 0, :CAP].reshape(slots), me, got.reshape(slots, order, width), nc * RB_DEV)
    sketch, gram_one = col_sum(term, own, nr, nc)
    upper_one, once, gram_part = first_pass(gram_one, sketch)
    gram_two = gram_sum(gram_part, nr, nc)
    scale = float(nr * nc * RB_DEV * order) ** 0.5
    return last_pass(gram_two, once, upper_one, scale)


def solution(mesh):
    nr, nc = mesh.shape["row"], mesh.shape["col"]
    return jax.shard_map(
        functools.partial(body, nr, nc),
        mesh=mesh,
        in_specs=(
            P(("row", "col"), None, None, None),
            P("col", None),
            P(("row", "col"), None),
            P(("row", "col")),
            P(("row", "col"), None),
        ),
        out_specs=(P(("row", "col"), None), P()),
        check_vma=False,
    )
```

time: 587 us -> 194 us (0.33); the launches traced: 578 us -> 193 us
  waiting for transfers between devices: 356 us -> 0 us
  Pallas kernels: 0 us -> 182 us
  other arithmetic: 117 us -> 1.71 us
  local copies, waits for them, and re-layouts: 43.4 us -> 8.58 us
  matrix products: 34.5 us -> 0 us
  between operations: 17.1 us -> 0.72 us
  starting transfers between devices: 9.61 us -> 0 us
    psum x2 -> x0, waiting for transfers between devices: 255 us -> none  [the longest x1 129 us: body(): gram_one = lax.psum(product(sketch.T, sketch), ('row', 'col'))]
    pallas_call x0 -> x7, Pallas kernels: none -> 182 us  [the longest x1 66.9 us: col_sum(): pl.pallas_call(functools.partial(col_sum_kernel, nr, nc), out_shape=(jax....]
    another operation x18 -> x0, other arithmetic: 110 us -> none  [the longest x13 68.8 us: upper_factor(): lower = jnp.linalg.cholesky(gram)]
    reduce_scatter x1 -> x0, waiting for transfers between devices: 76.3 us -> none  [body(): lax.psum_scatter(term.reshape(count, sketch_width), 'col', scatter_dimens...]
    dot_general x7 -> x0, matrix products: 31 us -> none  [the longest x1 19.5 us: body(): jnp.einsum('tgij,tgjk->tik', a_blocks, picked, preferred_element_type=jnp...]
    all_to_all x2 -> x0, waiting for transfers between devices: 25.3 us -> none  [the longest x1 25.3 us: body(): lax.all_to_all(send_values, 'row', split_axis=0, concat_axis=0, tiled=True)]
    gather x3 -> x0, local copies, waits for them, and re-layouts: 20 us -> none  [the longest x1 16.1 us: body(): picked = slab[col_target]]
    another operation x19 -> x1, local copies, waits for them, and re-layouts: 9.97 us -> 0.08 us  [body(): got_rows[:, 0, :CAP].reshape(slots)]
  transfers between devices with their start and end apart: 5 -> 0, of which waited for: 4 -> 0; matrix products, arithmetic and copies ran while one was open for 7% -> 0% of each run, Pallas kernels for 0% -> 0%
where the time goes in v1:
time: 194 us; the launch traced here: 193 us
  Pallas kernels  182 us (94%)
  local copies, waits for them, and re-layouts  8.58 us (4%)
    pallas_call x1, Pallas kernels, col_sum(): pl.pallas_call(functools.partial(col_sum_kernel, nr, nc), out_shape=(jax....  66.9 us
    pallas_call x1, Pallas kernels, first_pass(): pl.pallas_call(first_kernel, out_shape=(square, jax.ShapeDtypeStruct(sket...  28.9 us
    pallas_call x1, Pallas kernels, row_exchange(): pl.pallas_call(functools.partial(row_exchange_kernel, nr), out_shape=(jax...  27.9 us
    pallas_call x1, Pallas kernels, last_pass(): pl.pallas_call(functools.partial(last_kernel, scale), out_shape=(jax.Shap...  27.3 us
    pallas_call x1, Pallas kernels, gram_sum(): pl.pallas_call(functools.partial(gram_sum_kernel, nr, nc), out_shape=jax....  17.3 us
    pallas_call x1, Pallas kernels, partials(): pl.pallas_call(partial_kernel, out_shape=jax.ShapeDtypeStruct((slots, ord...  11.7 us
    unnamed x11, local copies, waits for them, and re-layouts  6.94 us

profile of v1, /device:TPU:0, one launch (start us, length us, event | category | flops | bytes accessed | tf_op | source)
XLA Modules:
  0.0 193.1 jit_solution(13629265608153431304)
XLA Ops:
  0.6 0.9 convert_reduce_fusion
  1.5 0.7 multiply_add_fusion
  2.2 0.1 select_reduce_fusion
  2.3 0.1 sub.7
  2.4 0.8 copy.8
  3.2 0.1 reshape.40.col_ref
  3.3 0.6 broadcast_in_dim.27.srow_ref
  3.9 0.0 copy-start.1
  3.9 1.6 copy-done.1
  5.5 11.7 %shard_map.68 = bf16[32,128,256]{2,1,0:T(8,128)(2,1)S(1)} custom-call(s32[32]{0:T(128)S(1)} %get-tuple-element.20.slot_ref, s32[512]{0:T(512)S(1)} %reshape.40.col_ref, bf16[32,16,128,128]{3,2,1,0:T(8,128)(2,1)} %a_ref.1, bf16[4096,256]{1,0:T(8,128)(2,1)S(1)} %copy-done.1), custom_call_target="tpu_custom_call" | custom-call | tf_op jit(solution)/shard_map/pallas_call | solution.py:52
  17.2 0.0 copy-start
  17.2 1.3 copy-done
  18.6 27.9 %shard_map.69 = (bf16[8,4,128,256]{3,2,1,0:T(8,128)(2,1)}, s32[8,8,128]{2,1,0:T(8,128)}) custom-call(bf16[8,4,128,256]{3,2,1,0:T(8,128)(2,1)} %bitcast.7, s32[8,8,128]{2,1,0:T(8,128)} %broadcast_in_dim.27.srow_ref), custom_call_target="tpu_custom_call" | custom-call | tf_op jit(solution)/shard_map/pallas_call | solution.py:94
  46.4 0.8 slice_reduce_fusion
  47.2 0.1 reshape_squeeze.3.rows_ref
  47.3 0.0 copy-start.2
  47.3 1.6 copy-done.2
  48.9 2.0 %shard_map.70 = (bf16[32,128,256]{2,1,0:T(8,128)(2,1)S(1)}, f32[8,128,256]{2,1,0:T(8,128)S(1)}) custom-call(s32[32]{0:T(128)S(1)} %reshape_squeeze.3.rows_ref, s32[1]{0:T(128)} %bitcast.3.me_ref, bf16[32,128,256]{2,1,0:T(8,128)(2,1)S(1)} %bitcast.8), custom_call_target="tpu_custom_call" | custom-call | tf_op jit(solution)/shard_map/pallas_call | solution.py:126
  50.9 66.9 %shard_map.71 = (f32[1024,256]{1,0:T(8,128)S(1)}, f32[256,256]{1,0:T(8,128)S(1)}) custom-call(bf16[32,128,256]{2,1,0:T(8,128)(2,1)S(1)} %get-tuple-element.13.term_ref, f32[8,128,256]{2,1,0:T(8,128)S(1)} %get-tuple-element.14.own_ref), custom_call_target="tpu_custom_call" | custom-call | tf_op jit(solution)/shard_map/pallas_call | solution.py:238
  117.8 28.9 %shard_map.72 = (f32[256,256]{1,0:T(8,128)S(1)}, f32[1024,256]{1,0:T(8,128)S(1)}, f32[256,256]{1,0:T(8,128)S(1)}) custom-call(f32[256,256]{1,0:T(8,128)S(1)} %get-tuple-element.15.gram, f32[1024,256]{1,0:T(8,128)S(1)} %get-tuple-element.16.sketch), custom_call_target="tpu_custom_call" | custom-call | tf_op jit(solution)/shard_map/pallas_call | solution.py:340
  146.8 0.0 copy-start.4
  146.8 0.7 copy-done.4
  147.5 17.3 %shard_map.73.gram = f32[256,256]{1,0:T(8,128)} custom-call(f32[256,256]{1,0:T(8,128)} %copy-done.4), custom_call_target="tpu_custom_call" | custom-call | tf_op jit(solution)/shard_map/pallas_call | solution.py:263
  164.8 0.0 copy-start.3
  164.8 0.9 copy-done.3
  165.7 27.3 %shard_map.74 = (f32[1024,256]{1,0:T(8,128)}, f32[256,256]{1,0:T(8,128)}) custom-call(f32[256,256]{1,0:T(8,128)S(1)} %copy-done.3, f32[1024,256]{1,0:T(8,128)S(1)} %get-tuple-element.18.once, f32[256,256]{1,0:T(8,128)S(1)} %get-tuple-element.19.upper_one), custom_call_target="tpu_custom_call" | custom-call | tf_op jit(solution)/shard_map/pallas_call | solution.py:364
  (2 shorter events, 0.0 us)
Async XLA Ops:
  3.9 1.6 copy-start.1
  17.2 1.3 copy-start
  47.3 1.6 copy-start.2
  146.8 0.7 copy-start.4
  164.8 1.0 copy-start.3

commit v2 on v1

--- a/solution.py
+++ b/solution.py
@@ -10,6 +10,8 @@
 RB_DEV = 8
 CAP = 4
 PANEL = 64
+HALVES = 2
+WIDE = 4
 MESH = pl.DeviceIdType.MESH
 ANY = pl.BlockSpec(memory_space=pl.ANY)
 VMEM = pl.BlockSpec(memory_space=pltpu.VMEM)
@@ -42,7 +44,10 @@
             right = jnp.concatenate([omega_ref[pl.ds(c0, order), :], omega_ref[pl.ds(c1, order), :]], axis=0)
             term = jnp.dot(left, right, preferred_element_type=jnp.float32)
             total = term if total is None else total + term
-        out_ref[slot_ref[t]] = total.astype(jnp.bfloat16)
+        total = total.astype(jnp.bfloat16)
+        half = out_ref.shape[-1]
+        for h in range(HALVES):
+            out_ref[h, slot_ref[t]] = total[:, h * half:(h + 1) * half]
 
 
 def partials(slot_of, col_flat, a_blocks, omega, slots):
@@ -51,7 +56,7 @@
     per_step = 4
     return pl.pallas_call(
         partial_kernel,
-        out_shape=jax.ShapeDtypeStruct((slots, order, width), jnp.bfloat16),
+        out_shape=jax.ShapeDtypeStruct((HALVES, slots, order, width // HALVES), jnp.bfloat16),
         grid_spec=pltpu.PrefetchScalarGridSpec(
             num_scalar_prefetch=2,
             grid=(targets // per_step,),
@@ -59,7 +64,7 @@
                 pl.BlockSpec((per_step, groups, order, order), lambda i, *_: (i, 0, 0, 0)),
                 pl.BlockSpec(omega.shape, lambda i, *_: (0, 0)),
             ],
-            out_specs=pl.BlockSpec((slots, order, width), lambda i, *_: (0, 0, 0)),
+            out_specs=pl.BlockSpec((HALVES, slots, order, width // HALVES), lambda i, *_: (0, 0, 0, 0)),
         ),
         compiler_params=pltpu.CompilerParams(vmem_limit_bytes=40 << 20),
     )(slot_of, col_flat, a_blocks, omega)
@@ -71,7 +76,7 @@
     barrier = pltpu.get_barrier_semaphore()
     for k in range(1, nr):
         pl.semaphore_signal(barrier, inc=1, device_id=(lax.rem(r + k, nr), c), device_id_type=MESH)
-    own = pltpu.make_async_copy(send_ref.at[r], got_ref.at[r], own_sem.at[0])
+    own = pltpu.make_async_copy(send_ref.at[0, r], got_ref.at[r], own_sem.at[0])
     own_rows = pltpu.make_async_copy(srow_ref.at[r], grow_ref.at[r], own_sem.at[1])
     own.start()
     own_rows.start()
@@ -79,7 +84,7 @@
     copies = []
     for k in range(1, nr):
         d = lax.rem(r + k, nr)
-        for src, dst, ss, rs in ((srow_ref, grow_ref, s2_sem, r2_sem), (send_ref, got_ref, s_sem, r_sem)):
+        for src, dst, ss, rs in ((srow_ref, grow_ref, s2_sem, r2_sem), (send_ref.at[0], got_ref, s_sem, r_sem)):
             cp = pltpu.make_async_remote_copy(src.at[d], dst.at[r], ss.at[k], rs.at[k], device_id=(d, c), device_id_type=MESH)
             cp.start()
             copies.append(cp)
@@ -93,12 +98,51 @@
     dma = pltpu.SemaphoreType.DMA
     return pl.pallas_call(
         functools.partial(row_exchange_kernel, nr),
-        out_shape=(jax.ShapeDtypeStruct(send.shape, send.dtype), jax.ShapeDtypeStruct(rows.shape, rows.dtype)),
+        out_shape=(jax.ShapeDtypeStruct(send.shape[1:], send.dtype), jax.ShapeDtypeStruct(rows.shape, rows.dtype)),
         in_specs=[ANY, ANY],
         out_specs=(ANY, ANY),
         scratch_shapes=[dma((nr,)), dma((nr,)), dma((nr,)), dma((nr,)), dma((2,))],
         compiler_params=pltpu.CompilerParams(collective_id=1, has_side_effects=True),
     )(send, rows)
+
+
+def both_exchange_kernel(nr, nc, send_ref, term_ref, got_ref, arrived_ref, s_sem, r_sem, s2_sem, r2_sem, own_sem):
+    r = lax.axis_index("row")
+    c = lax.axis_index("col")
+    own = pltpu.make_async_copy(send_ref.at[1, r], got_ref.at[r], own_sem.at[0])
+    own.start()
+    greet(nr, nc, r, c)
+    copies = []
+    for k in range(1, nc):
+        d = lax.rem(c + k, nc)
+        copies.append(pltpu.make_async_remote_copy(
+            term_ref.at[pl.ds(d * RB_DEV, RB_DEV)], arrived_ref.at[k], s2_sem.at[k], r2_sem.at[k],
+            device_id=(r, d), device_id_type=MESH))
+        copies[-1].start()
+    for k in range(1, nr):
+        d = lax.rem(r + k, nr)
+        copies.append(pltpu.make_async_remote_copy(
+            send_ref.at[1, d], got_ref.at[r], s_sem.at[k], r_sem.at[k], device_id=(d, c), device_id_type=MESH))
+        copies[-1].start()
+    own.wait()
+    for cp in copies:
+        cp.wait()
+
+
+def both_exchange(send, term, nr, nc):
+    dma = pltpu.SemaphoreType.DMA
+    _, order, width = term.shape
+    return pl.pallas_call(
+        functools.partial(both_exchange_kernel, nr, nc),
+        out_shape=(
+            jax.ShapeDtypeStruct(send.shape[1:], send.dtype),
+            jax.ShapeDtypeStruct((nc, RB_DEV, order, width), term.dtype),
+        ),
+        in_specs=[ANY, ANY],
+        out_specs=(ANY, ANY),
+        scratch_shapes=[dma((nr,)), dma((nr,)), dma((nc,)), dma((nc,)), dma((1,))],
+        compiler_params=pltpu.CompilerParams(collective_id=4, has_side_effects=True),
+    )(send, term)
 
 
 def gather_sum_kernel(rows_ref, me_ref, got_ref, term_ref, own_ref, acc):
@@ -197,7 +241,7 @@
     ]
 
 
-def col_sum_kernel(nr, nc, term_ref, own_ref, sketch_ref, out_ref, got, gram, landed, cols, full, *sems):
+def col_sum_kernel(nr, nc, term_ref, own_ref, arrived0, own0, sketch_ref, out_ref, got, gram, landed, cols, full, *sems):
     r = lax.axis_index("row")
     c = lax.axis_index("col")
     s_sem, r_sem = sems[6], sems[7]
@@ -220,10 +264,11 @@
         pieces = []
         for half in range(2):
             b = i * 2 + half
-            total = own_ref[b]
+            total0, total1 = own0[b], own_ref[b]
             for k in range(1, nc):
-                total = total + got[k, b].astype(jnp.float32)
-            pieces.append(total)
+                total0 = total0 + arrived0[k, b].astype(jnp.float32)
+                total1 = total1 + got[k, b].astype(jnp.float32)
+            pieces.append(jnp.concatenate([total0, total1], axis=1))
         rows = jnp.concatenate(pieces, axis=0)
         sketch_ref[pl.ds(pl.multiple_of(i * 2 * order, 2 * order), 2 * order), :] = rows
         gram[...] += dot_tn(rows, rows)
@@ -232,8 +277,9 @@
     out_ref[...] = full[...]
 
 
-def col_sum(term, own, nr, nc):
-    _, order, width = own.shape
+def col_sum(term, own, arrived0, own0, nr, nc):
+    _, order, half = own.shape
+    width = HALVES * half
     dma = pltpu.SemaphoreType.DMA
     return pl.pallas_call(
         functools.partial(col_sum_kernel, nr, nc),
@@ -241,14 +287,14 @@
             jax.ShapeDtypeStruct((RB_DEV * order, width), jnp.float32),
             jax.ShapeDtypeStruct((width, width), jnp.float32),
         ),
-        in_specs=[VMEM, VMEM],
+        in_specs=[VMEM, VMEM, VMEM, VMEM],
         out_specs=(VMEM, VMEM),
         scratch_shapes=[
-            pltpu.VMEM((nc, RB_DEV, order, width), jnp.bfloat16),
+            pltpu.VMEM((nc, RB_DEV, order, half), jnp.bfloat16),
             pltpu.VMEM((width, width), jnp.float32),
         ] + gram_scratch(nr, nc, width) + [dma((nc,)), dma((nc,))],
         compiler_params=pltpu.CompilerParams(collective_id=2, has_side_effects=True, vmem_limit_bytes=48 << 20),
-    )(term, own)
+    )(term, own, arrived0, own0)
 
 
 def gram_sum_kernel(nr, nc, gram, out_ref, landed, cols, full, *sems):
@@ -272,19 +318,36 @@
 
 def eliminate(x):
     rows = x.shape[0]
+    shape = (8, x.shape[1])
     groups = [x[i:i + 8, :] for i in range(0, rows, 8)]
-    sub = lax.broadcasted_iota(jnp.int32, (8, 1), 0)
-    for j in range(rows - 1):
+    sub = lax.broadcasted_iota(jnp.int32, shape, 0)
+    for j in range(0, rows, WIDE):
         g, o = divmod(j, 8)
-        pivot_row = groups[g][o:o + 1, :]
-        scaled = pivot_row * (1.0 / pivot_row[:, j:j + 1])
+        cols = [[jnp.broadcast_to(groups[i][:, j + l:j + l + 1], shape) for l in range(WIDE)]
+                for i in range(g, rows // 8)]
+        piv = [[jnp.broadcast_to(cols[0][l][o + k:o + k + 1, :], shape) for l in range(WIDE)] for k in range(WIDE)]
+        tops = [jnp.broadcast_to(groups[g][o + k:o + k + 1, :], shape) for k in range(WIDE)]
+        recip = []
+        for k in range(WIDE):
+            recip.append(1.0 / piv[k][k])
+            for m in range(k + 1, WIDE):
+                q = piv[m][k] * recip[k]
+                for l in range(k + 1, WIDE):
+                    piv[m][l] = piv[m][l] - q * piv[k][l]
+                tops[m] = tops[m] - q * tops[k]
         for i in range(g, rows // 8):
-            f = groups[i][:, j:j + 1]
+            here = cols[i - g]
+            value = groups[i]
+            for k in range(WIDE):
+                f = here[k] * recip[k]
+                for l in range(k + 1, WIDE):
+                    here[l] = here[l] - f * piv[k][l]
+                value = value - f * tops[k]
             if i == g:
-                if o == 7:
-                    continue
-                f = jnp.where(sub > o, f, 0.0)
-            groups[i] = groups[i] - f * scaled
+                value = jnp.where(sub >= o + WIDE, value, groups[i])
+                for k in range(1, WIDE):
+                    value = jnp.where(sub == o + k, tops[k], value)
+            groups[i] = value
     return jnp.concatenate(groups, axis=0)
 
 
@@ -390,10 +453,15 @@
     send_rows = jnp.pad(send_rows.reshape(nr, 1, CAP), ((0, 0), (0, 0), (0, 128 - CAP)))
     send_rows = jnp.broadcast_to(send_rows, (nr, 8, 128))
     send = partials(slot_of, col_target.reshape(-1), a_blocks, omega, slots)
-    got, got_rows = row_exchange(send.reshape(nr, CAP, order, width), send_rows, nr)
+    half = width // HALVES
+    send = send.reshape(HALVES, nr, CAP, order, half)
+    got0, got_rows = row_exchange(send, send_rows, nr)
     me = lax.axis_index("col").astype(jnp.int32).reshape(1)
-    term, own = gather_sum(got_rows[:, 0, :CAP].reshape(slots), me, got.reshape(slots, order, width), nc * RB_DEV)
-    sketch, gram_one = col_sum(term, own, nr, nc)
+    rows = got_rows[:, 0, :CAP].reshape(slots)
+    term0, own0 = gather_sum(rows, me, got0.reshape(slots, order, half), nc * RB_DEV)
+    got1, arrived0 = both_exchange(send, term0, nr, nc)
+    term1, own1 = gather_sum(rows, me, got1.reshape(slots, order, half), nc * RB_DEV)
+    sketch, gram_one = col_sum(term1, own1, arrived0, own0, nr, nc)
     upper_one, once, gram_part = first_pass(gram_one, sketch)
     gram_two = gram_sum(gram_part, nr, nc)
     scale = float(nr * nc * RB_DEV * order) ** 0.5

time: 194 us -> 169 us (0.87)
  Pallas kernels: 182 us -> 155 us
  local copies, waits for them, and re-layouts: 8.58 us -> 11.6 us
    pallas_call x1 -> x2, Pallas kernels: 11.7 us -> 36.2 us  [the longest x1 24.4 us: both_exchange(): pl.pallas_call(functools.partial(both_exchange_kernel, nr, nc), out_shape...]
    pallas_call x1, Pallas kernels: 66.9 us -> 44.9 us  [col_sum(): pl.pallas_call(functools.partial(col_sum_kernel, nr, nc), out_shape=(jax....]
    pallas_call x1, Pallas kernels: 27.9 us -> 16.6 us  [row_exchange(): pl.pallas_call(functools.partial(row_exchange_kernel, nr), out_shape=(jax...]
    pallas_call x1, Pallas kernels: 28.9 us -> 18.9 us  [first_pass(): pl.pallas_call(first_kernel, out_shape=(square, jax.ShapeDtypeStruct(sket...]
    pallas_call x1, Pallas kernels: 27.3 us -> 17.3 us  [last_pass(): pl.pallas_call(functools.partial(last_kernel, scale), out_shape=(jax.Shap...]
    unnamed x11 -> x17, local copies, waits for them, and re-layouts: 6.94 us -> 9.99 us
where the time goes in v2:
time: 169 us
  Pallas kernels  155 us (92%)
  local copies, waits for them, and re-layouts  11.6 us (7%)
  other arithmetic  1.71 us (1%)
    pallas_call x1, Pallas kernels, col_sum(): pl.pallas_call(functools.partial(col_sum_kernel, nr, nc), out_shape=(jax....  44.9 us
    pallas_call x1, Pallas kernels, both_exchange(): pl.pallas_call(functools.partial(both_exchange_kernel, nr, nc), out_shape...  24.4 us
    pallas_call x1, Pallas kernels, first_pass(): pl.pallas_call(first_kernel, out_shape=(square, jax.ShapeDtypeStruct(sket...  18.9 us
    pallas_call x1, Pallas kernels, gram_sum(): pl.pallas_call(functools.partial(gram_sum_kernel, nr, nc), out_shape=jax....  17.5 us
    pallas_call x1, Pallas kernels, last_pass(): pl.pallas_call(functools.partial(last_kernel, scale), out_shape=(jax.Shap...  17.3 us
    pallas_call x1, Pallas kernels, row_exchange(): pl.pallas_call(functools.partial(row_exchange_kernel, nr), out_shape=(jax...  16.6 us
    pallas_call x1, Pallas kernels, partials(): pl.pallas_call(partial_kernel, out_shape=jax.ShapeDtypeStruct((HALVES, sl...  11.8 us
    unnamed x17, local copies, waits for them, and re-layouts  9.99 us

profile of v2, /device:TPU:0, one launch (start us, length us, event | category | flops | bytes accessed | tf_op | source)
XLA Modules:
  0.0 168.7 jit_solution(5928929599145347223)
XLA Ops:
  0.6 0.9 convert_reduce_fusion
  1.5 0.7 multiply_add_fusion
  2.2 0.1 select_reduce_fusion
  2.3 0.1 sub.7
  2.4 0.8 copy.8
  3.2 0.1 reshape.43.col_ref
  3.3 0.6 broadcast_in_dim.27.srow_ref
  3.9 0.0 copy-start.1
  3.9 1.6 copy-done.1
  5.5 11.8 %shard_map.68 = bf16[2,32,128,128]{3,2,1,0:T(8,128)(2,1)S(1)} custom-call(s32[32]{0:T(128)S(1)} %get-tuple-element.28.slot_ref, s32[512]{0:T(512)S(1)} %reshape.43.col_ref, bf16[32,16,128,128]{3,2,1,0:T(8,128)(2,1)} %a_ref.1, bf16[4096,256]{1,0:T(8,128)(2,1)S(1)} %copy-done.1), custom_call_target="tpu_custom_call" | custom-call | tf_op jit(solution)/shard_map/pallas_call | solution.py:57
  17.3 0.0 copy-start
  17.3 1.3 copy-done
  18.7 16.6 %shard_map.69 = (bf16[8,4,128,128]{3,2,1,0:T(8,128)(2,1)}, s32[8,8,128]{2,1,0:T(8,128)}) custom-call(bf16[2,8,4,128,128]{4,3,2,1,0:T(8,128)(2,1)} %bitcast.8, s32[8,8,128]{2,1,0:T(8,128)} %broadcast_in_dim.27.srow_ref), custom_call_target="tpu_custom_call" | custom-call | tf_op jit(solution)/shard_map/pallas_call | solution.py:99
  35.3 0.8 slice_reduce_fusion
  36.1 0.1 reshape_squeeze.3.rows_ref
  36.2 0.0 copy-start.4
  36.2 1.2 copy-done.4
  37.4 1.6 shard_map.70
  39.0 0.0 copy-start.3
  39.0 1.0 copy-done.3
  40.0 24.4 %shard_map.71 = (bf16[8,4,128,128]{3,2,1,0:T(8,128)(2,1)}, bf16[4,8,128,128]{3,2,1,0:T(8,128)(2,1)}) custom-call(bf16[2,8,4,128,128]{4,3,2,1,0:T(8,128)(2,1)} %bitcast.9, bf16[32,128,128]{2,1,0:T(8,128)(2,1)} %copy-done.3), custom_call_target="tpu_custom_call" | custom-call | tf_op jit(solution)/shard_map/pallas_call | solution.py:135
  64.3 0.0 copy-start.5
  64.3 1.2 copy-done.5
  65.6 1.6 shard_map.72
  67.1 0.0 copy-start.2
  67.1 1.2 copy-done.2
  68.4 44.9 %shard_map.73 = (f32[1024,256]{1,0:T(8,128)S(1)}, f32[256,256]{1,0:T(8,128)S(1)}) custom-call(bf16[32,128,128]{2,1,0:T(8,128)(2,1)S(1)} %get-tuple-element.19.term_ref, f32[8,128,128]{2,1,0:T(8,128)S(1)} %get-tuple-element.20.own_ref, bf16[4,8,128,128]{3,2,1,0:T(8,128)(2,1)S(1)} %copy-done.2, f32[8,128,128]{2,1,0:T(8,128)S(1)} %get-tuple-element.22.own0), custom_call_target="tpu_custom_call" | custom-call | tf_op jit(solution)/shard_map/pallas_call | solution.py:284
  113.3 18.9 %shard_map.74 = (f32[256,256]{1,0:T(8,128)S(1)}, f32[1024,256]{1,0:T(8,128)S(1)}, f32[256,256]{1,0:T(8,128)S(1)}) custom-call(f32[256,256]{1,0:T(8,128)S(1)} %get-tuple-element.23.gram, f32[1024,256]{1,0:T(8,128)S(1)} %get-tuple-element.24.sketch), custom_call_target="tpu_custom_call" | custom-call | tf_op jit(solution)/shard_map/pallas_call | solution.py:403
  132.2 0.0 copy-start.7
  132.2 0.7 copy-done.7
  132.9 17.5 %shard_map.75.gram = f32[256,256]{1,0:T(8,128)} custom-call(f32[256,256]{1,0:T(8,128)} %copy-done.7), custom_call_target="tpu_custom_call" | custom-call | tf_op jit(solution)/shard_map/pallas_call | solution.py:309
  150.4 0.0 copy-start.6
  150.4 0.9 copy-done.6
  151.4 17.3 %shard_map.76 = (f32[1024,256]{1,0:T(8,128)}, f32[256,256]{1,0:T(8,128)}) custom-call(f32[256,256]{1,0:T(8,128)S(1)} %copy-done.6, f32[1024,256]{1,0:T(8,128)S(1)} %get-tuple-element.26.once, f32[256,256]{1,0:T(8,128)S(1)} %get-tuple-element.27.upper_one), custom_call_target="tpu_custom_call" | custom-call | tf_op jit(solution)/shard_map/pallas_call | solution.py:427
  (2 shorter events, 0.0 us)
Async XLA Ops:
  3.9 1.6 copy-start.1
  17.3 1.4 copy-start
  36.2 1.2 copy-start.4
  39.0 1.0 copy-start.3
  64.3 1.2 copy-start.5
  67.1 1.2 copy-start.2
  132.2 0.7 copy-start.7
  150.4 1.0 copy-start.6

commit v3 on v2

--- a/solution.py
+++ b/solution.py
@@ -13,7 +13,6 @@
 HALVES = 2
 WIDE = 4
 MESH = pl.DeviceIdType.MESH
-ANY = pl.BlockSpec(memory_space=pl.ANY)
 VMEM = pl.BlockSpec(memory_space=pltpu.VMEM)
 SMEM = pl.BlockSpec(memory_space=pltpu.SMEM)
 HIGH = lax.Precision.HIGHEST
@@ -66,7 +65,7 @@
             ],
             out_specs=pl.BlockSpec((HALVES, slots, order, width // HALVES), lambda i, *_: (0, 0, 0, 0)),
         ),
-        compiler_params=pltpu.CompilerParams(vmem_limit_bytes=40 << 20),
+        compiler_params=pltpu.CompilerParams(vmem_limit_bytes=50 << 20),
     )(slot_of, col_flat, a_blocks, omega)
 
 
@@ -99,10 +98,10 @@
     return pl.pallas_call(
         functools.partial(row_exchange_kernel, nr),
         out_shape=(jax.ShapeDtypeStruct(send.shape[1:], send.dtype), jax.ShapeDtypeStruct(rows.shape, rows.dtype)),
-        in_specs=[ANY, ANY],
-        out_specs=(ANY, ANY),
+        in_specs=[VMEM, VMEM],
+        out_specs=(VMEM, VMEM),
         scratch_shapes=[dma((nr,)), dma((nr,)), dma((nr,)), dma((nr,)), dma((2,))],
-        compiler_params=pltpu.CompilerParams(collective_id=1, has_side_effects=True),
+        compiler_params=pltpu.CompilerParams(collective_id=1, has_side_effects=True, vmem_limit_bytes=16 << 20),
     )(send, rows)
 
 
@@ -138,10 +137,10 @@
             jax.ShapeDtypeStruct(send.shape[1:], send.dtype),
             jax.ShapeDtypeStruct((nc, RB_DEV, order, width), term.dtype),
         ),
-        in_specs=[ANY, ANY],
-        out_specs=(ANY, ANY),
+        in_specs=[VMEM, VMEM],
+        out_specs=(VMEM, VMEM),
         scratch_shapes=[dma((nr,)), dma((nr,)), dma((nc,)), dma((nc,)), dma((1,))],
-        compiler_params=pltpu.CompilerParams(collective_id=4, has_side_effects=True),
+        compiler_params=pltpu.CompilerParams(collective_id=4, has_side_effects=True, vmem_limit_bytes=16 << 20),
     )(send, term)
 
 
@@ -176,7 +175,7 @@
         in_specs=[SMEM, SMEM, VMEM],
         out_specs=(VMEM, VMEM),
         scratch_shapes=[pltpu.VMEM((blocks, order, width), jnp.float32)],
-        compiler_params=pltpu.CompilerParams(vmem_limit_bytes=48 << 20),
+        compiler_params=pltpu.CompilerParams(vmem_limit_bytes=20 << 20),
     )(rows, me, got)
 
 
@@ -254,25 +253,39 @@
             device_id=(r, d), device_id_type=MESH)
         cp.start()
         copies.append(cp)
-    for cp in copies:
-        cp.wait()
-    order = own_ref.shape[1]
+    _, order, half = own_ref.shape
     gram[...] = jnp.zeros_like(gram)
+    pair = 2 * order
 
     @pl.loop(0, RB_DEV // 2)
     def _(i):
         pieces = []
-        for half in range(2):
-            b = i * 2 + half
-            total0, total1 = own0[b], own_ref[b]
+        for b in (2 * i, 2 * i + 1):
+            total = own0[b]
             for k in range(1, nc):
-                total0 = total0 + arrived0[k, b].astype(jnp.float32)
-                total1 = total1 + got[k, b].astype(jnp.float32)
-            pieces.append(jnp.concatenate([total0, total1], axis=1))
+                total = total + arrived0[k, b].astype(jnp.float32)
+            pieces.append(total)
         rows = jnp.concatenate(pieces, axis=0)
-        sketch_ref[pl.ds(pl.multiple_of(i * 2 * order, 2 * order), 2 * order), :] = rows
-        gram[...] += dot_tn(rows, rows)
-
+        sketch_ref[pl.ds(pl.multiple_of(i * pair, pair), pair), :half] = rows
+        gram[:half, :half] += dot_tn(rows, rows)
+
+    for cp in copies:
+        cp.wait()
+
+    @pl.loop(0, RB_DEV // 2)
+    def _(i):
+        pieces = []
+        for b in (2 * i, 2 * i + 1):
+            total = own_ref[b]
+            for k in range(1, nc):
+                total = total + got[k, b].astype(jnp.float32)
+            pieces.append(total)
+        rows = jnp.concatenate(pieces, axis=0)
+        part = pl.ds(pl.multiple_of(i * pair, pair), pair)
+        sketch_ref[part, half:] = rows
+        gram[:, half:] += dot_tn(sketch_ref[part, :], rows)
+
+    gram[half:, :half] = gram[:half, half:].T
     reduce_gram(nr, nc, r, c, gram, landed, cols, full, sems[:6])
     out_ref[...] = full[...]
 
@@ -293,7 +306,7 @@
             pltpu.VMEM((nc, RB_DEV, order, half), jnp.bfloat16),
             pltpu.VMEM((width, width), jnp.float32),
         ] + gram_scratch(nr, nc, width) + [dma((nc,)), dma((nc,))],
-        compiler_params=pltpu.CompilerParams(collective_id=2, has_side_effects=True, vmem_limit_bytes=48 << 20),
+        compiler_params=pltpu.CompilerParams(collective_id=2, has_side_effects=True, vmem_limit_bytes=24 << 20),
     )(term, own, arrived0, own0)
 
 
@@ -312,7 +325,7 @@
         in_specs=[VMEM],
         out_specs=VMEM,
         scratch_shapes=gram_scratch(nr, nc, gram.shape[0]),
-        compiler_params=pltpu.CompilerParams(collective_id=3, has_side_effects=True),
+        compiler_params=pltpu.CompilerParams(collective_id=3, has_side_effects=True, vmem_limit_bytes=8 << 20),
     )(gram)
 
 
@@ -406,7 +419,7 @@
         in_specs=[VMEM, VMEM],
         out_specs=(VMEM, VMEM, VMEM),
         scratch_shapes=[pltpu.VMEM((order, 2 * order), jnp.float32), pltpu.VMEM((order, order), jnp.float32)],
-        compiler_params=pltpu.CompilerParams(vmem_limit_bytes=40 << 20),
+        compiler_params=pltpu.CompilerParams(vmem_limit_bytes=16 << 20),
     )(gram, sketch)
 
 
@@ -433,7 +446,7 @@
         in_specs=[VMEM, VMEM, VMEM],
         out_specs=(VMEM, VMEM),
         scratch_shapes=[pltpu.VMEM((order, 2 * order), jnp.float32), square, square],
-        compiler_params=pltpu.CompilerParams(vmem_limit_bytes=40 << 20),
+        compiler_params=pltpu.CompilerParams(vmem_limit_bytes=16 << 20),
     )(gram, once, upper_one)
 
 

time: 169 us -> 157 us (0.929)
  local copies, waits for them, and re-layouts: 11.6 us -> 1.05 us
  Pallas kernels: 155 us -> 153 us
    unnamed x17 -> x1, local copies, waits for them, and re-layouts: 9.99 us -> 0.78 us
where the time goes in v3:
time: 157 us
  Pallas kernels  153 us (97%)
  other arithmetic  1.71 us (1%)
    pallas_call x1, Pallas kernels, col_sum(): pl.pallas_call(functools.partial(col_sum_kernel, nr, nc), out_shape=(jax....  45.1 us
    pallas_call x1, Pallas kernels, both_exchange(): pl.pallas_call(functools.partial(both_exchange_kernel, nr, nc), out_shape...  24.3 us
    pallas_call x1, Pallas kernels, first_pass(): pl.pallas_call(first_kernel, out_shape=(square, jax.ShapeDtypeStruct(sket...  18.9 us
    pallas_call x1, Pallas kernels, last_pass(): pl.pallas_call(functools.partial(last_kernel, scale), out_shape=(jax.Shap...  17.3 us
    pallas_call x1, Pallas kernels, row_exchange(): pl.pallas_call(functools.partial(row_exchange_kernel, nr), out_shape=(jax...  16.4 us
    pallas_call x1, Pallas kernels, gram_sum(): pl.pallas_call(functools.partial(gram_sum_kernel, nr, nc), out_shape=jax....  16.2 us
    pallas_call x1, Pallas kernels, partials(): pl.pallas_call(partial_kernel, out_shape=jax.ShapeDtypeStruct((HALVES, sl...  11.8 us

profile of v3, /device:TPU:0, one launch (start us, length us, event | category | flops | bytes accessed | tf_op | source)
XLA Modules:
  0.0 156.6 jit_solution(5917032354162362920)
XLA Ops:
  0.6 0.9 convert_reduce_fusion
  1.5 0.7 multiply_add_fusion
  2.2 0.1 select_reduce_fusion
  2.3 0.1 sub.7
  2.4 0.8 copy.8
  3.2 0.1 reshape.43.col_ref
  3.3 11.8 %shard_map.68 = bf16[2,32,128,128]{3,2,1,0:T(8,128)(2,1)S(1)} custom-call(s32[32]{0:T(128)S(1)} %get-tuple-element.28.slot_ref, s32[512]{0:T(512)S(1)} %reshape.43.col_ref, bf16[32,16,128,128]{3,2,1,0:T(8,128)(2,1)} %a_ref.1, bf16[4096,256]{1,0:T(8,128)(2,1)} %omega_ref.1), custom_call_target="tpu_custom_call" | custom-call | tf_op jit(solution)/shard_map/pallas_call | solution.py:56
  15.1 16.4 %shard_map.69 = (bf16[8,4,128,128]{3,2,1,0:T(8,128)(2,1)S(1)}, s32[8,8,128]{2,1,0:T(8,128)S(1)}) custom-call(bf16[2,8,4,128,128]{4,3,2,1,0:T(8,128)(2,1)S(1)} %bitcast.8, s32[8,8,128]{2,1,0:T(8,128)S(1)} %broadcast_in_dim.27.srow_ref), custom_call_target="tpu_custom_call" | custom-call | tf_op jit(solution)/shard_map/pallas_call | solution.py:98
  31.5 0.1 reshape_squeeze.3.rows_ref
  31.6 1.6 shard_map.70
  33.2 24.3 %shard_map.71 = (bf16[8,4,128,128]{3,2,1,0:T(8,128)(2,1)S(1)}, bf16[4,8,128,128]{3,2,1,0:T(8,128)(2,1)S(1)}) custom-call(bf16[2,8,4,128,128]{4,3,2,1,0:T(8,128)(2,1)S(1)} %bitcast.9, bf16[32,128,128]{2,1,0:T(8,128)(2,1)S(1)} %get-tuple-element.17.term_ref), custom_call_target="tpu_custom_call" | custom-call | tf_op jit(solution)/shard_map/pallas_call | solution.py:134
  57.5 1.6 shard_map.72
  59.0 45.1 %shard_map.73 = (f32[1024,256]{1,0:T(8,128)S(1)}, f32[256,256]{1,0:T(8,128)S(1)}) custom-call(bf16[32,128,128]{2,1,0:T(8,128)(2,1)S(1)} %get-tuple-element.19.term_ref, f32[8,128,128]{2,1,0:T(8,128)S(1)} %get-tuple-element.20.own_ref, bf16[4,8,128,128]{3,2,1,0:T(8,128)(2,1)S(1)} %get-tuple-element.21.arrived0, f32[8,128,128]{2,1,0:T(8,128)S(1)} %get-tuple-element.22.own0), custom_call_target="tpu_custom_call" | custom-call | tf_op jit(solution)/shard_map/pallas_call | solution.py:297
  104.2 18.9 %shard_map.74 = (f32[256,256]{1,0:T(8,128)S(1)}, f32[1024,256]{1,0:T(8,128)S(1)}, f32[256,256]{1,0:T(8,128)S(1)}) custom-call(f32[256,256]{1,0:T(8,128)S(1)} %get-tuple-element.23.gram, f32[1024,256]{1,0:T(8,128)S(1)} %get-tuple-element.24.sketch), custom_call_target="tpu_custom_call" | custom-call | tf_op jit(solution)/shard_map/pallas_call | solution.py:416
  123.1 16.2 %shard_map.75.gram = f32[256,256]{1,0:T(8,128)S(1)} custom-call(f32[256,256]{1,0:T(8,128)S(1)} %get-tuple-element.25.gram), custom_call_target="tpu_custom_call" | custom-call | tf_op jit(solution)/shard_map/pallas_call | solution.py:322
  139.3 17.3 %shard_map.76 = (f32[1024,256]{1,0:T(8,128)}, f32[256,256]{1,0:T(8,128)}) custom-call(f32[256,256]{1,0:T(8,128)S(1)} %shard_map.75.gram, f32[1024,256]{1,0:T(8,128)S(1)} %get-tuple-element.26.once, f32[256,256]{1,0:T(8,128)S(1)} %get-tuple-element.27.upper_one), custom_call_target="tpu_custom_call" | custom-call | tf_op jit(solution)/shard_map/pallas_call | solution.py:440
  (4 shorter events, 0.0 us)
